TPU v7x, 1024 devices: a whole 4x8x16 slice. The times are simulated.
1024 devices in a mesh: gx: 4 (over x), gy: 16 (over z_hi, y), gz: 16 (over z_lo, core).
Axes of the slice: x: 4, y: 8, z: 16 (z_hi: 2, z_lo: 8; z = z_hi * 8 + z_lo), core: 2. Of those that a mesh axis runs over, the one named last changes fastest.
Arguments:
- populations: float32 [19, 8, 256, 2048], P(None, 'gx', 'gy', 'gz'), may hold values from 0.1 to 12, as said below
- shear_rate: float32 [8, 256, 2048], P('gx', 'gy', 'gz'), may hold values from 1 to 1.9
- part_cell: int32 [8388608], P(('gx', 'gy', 'gz')), may hold values from 0 to 4095
- part_move: int32 [8388608], P(('gx', 'gy', 'gz')), may hold values from 0 to 6
- part_mask: int32 [8388608], P(('gx', 'gy', 'gz')), may hold values 0 or 1
- part_velocity: float32 [3, 8388608], P(None, ('gx', 'gy', 'gz')), may hold values from -6 to 6
- part_mass: float32 [8388608], P(('gx', 'gy', 'gz')), may hold values from 0.5 to 2
Outputs:
- populations_out: float32 [19, 8, 256, 2048], P(None, 'gx', 'gy', 'gz')
- sources: float32 [4, 8, 256, 2048], P(None, 'gx', 'gy', 'gz')
- velocity_out: float32 [3, 8388608], P(None, ('gx', 'gy', 'gz'))
Inputs may be any that keep to these rules, and one draw needn't show every extreme that they name: `populations`: each entry is a positive population; a node's 19 values sum to its density. `part_cell`: local index of the particle's cell in the brick of the device holding it, (x * 16 + y) * 128 + z. `part_move`: 0 stays; 1 and 2 move to the next node along +x and -x, 3 and 4 along +y and -y, 5 and 6 along +z and -z. `part_mask`: 1 marks a particle of the advanced subset.
All inputs are finite; a program needn't handle non-finite values. No bound on the sum of `part_mask` on one device may be relied on, other than what follows from the above.
Results may differ from a plain program's by a relative error of at most 0.0001.
Values sent between devices are 32-bit elements; how exact they have to be, the bound alone decides.
No kernel may reach another device: no remote copies, remote signals or barrier semaphores. Data moves between devices by JAX's collectives and lax.ppermute only.
A program may use at most 32 MiB of HBM per device.

v0:
```python
import functools

import jax
import jax.numpy as jnp
from jax import lax
from jax.experimental import pallas as pl
from jax.experimental.pallas import tpu as pltpu
from jax.sharding import PartitionSpec as P

SPEEDS = (
    (0, 0, 0),
    (1, 0, 0),
    (-1, 0, 0),
    (0, 1, 0),
    (0, -1, 0),
    (0, 0, 1),
    (0, 0, -1),
    (1, 1, 0),
    (-1, -1, 0),
    (1, -1, 0),
    (-1, 1, 0),
    (1, 0, 1),
    (-1, 0, -1),
    (1, 0, -1),
    (-1, 0, 1),
    (0, 1, 1),
    (0, -1, -1),
    (0, 1, -1),
    (0, -1, 1),
)
SHEAR = 19
UP = [i for i in range(19) if SPEEDS[i][0] == 1]
FLAT = [i for i in range(19) if SPEEDS[i][0] == 0]
DOWN = [i for i in range(19) if SPEEDS[i][0] == -1]
X_LOW = [(f, -1) for f in UP + FLAT + [SHEAR]] + [(f, -2) for f in UP]
X_HIGH = [(f, 2) for f in DOWN + FLAT + [SHEAR]] + [(f, 3) for f in DOWN]
PAIRS = X_LOW + [(f, 0) for f in range(20)] + [(f, 1) for f in range(20)] + X_HIGH
INDEX = {pair: q for q, pair in enumerate(PAIRS)}
FIRST = 42
DEP_LANE = 3 * (len(PAIRS) - FIRST)
Y_ROWS = 264
VMEM = pl.BlockSpec(memory_space=pltpu.VMEM)
SMEM = pl.BlockSpec(memory_space=pltpu.SMEM)
HBM = pl.BlockSpec(memory_space=pltpu.HBM)


def relax(f, shear):
    s1, s2, s3 = f[1] + f[2], f[3] + f[4], f[5] + f[6]
    d1, d2, d3 = f[1] - f[2], f[3] - f[4], f[5] - f[6]
    e1, e2, e3 = f[7] + f[8], f[9] + f[10], f[11] + f[12]
    e4, e5, e6 = f[13] + f[14], f[15] + f[16], f[17] + f[18]
    g1, g2, g3 = f[7] - f[8], f[9] - f[10], f[11] - f[12]
    g4, g5, g6 = f[13] - f[14], f[15] - f[16], f[17] - f[18]
    exy, exz, eyz = e1 + e2, e3 + e4, e5 + e6
    s23, m23 = s2 + s3, s2 - s3
    axes = s1 + s23
    exx = exy + exz
    edges = exx + eyz
    rho = f[0] + axes + edges
    gp, gm = g1 + g2, g1 - g2
    hp, hm = g3 + g4, g3 - g4
    kp, km = g5 + g6, g5 - g6
    gx, gy, gz = gp + hp, gm + kp, hm + km
    jx, jy, jz = d1 + gx, d2 + gy, d3 + gz
    inv = 1.0 / rho
    ux, uy, uz = jx * inv, jy * inv, jz * inv
    xx, yy, zz = jx * ux, jy * uy, jz * uz
    sq = xx + yy + zz
    n1 = 8.0 * edges - 11.0 * axes - 30.0 * f[0] + (11.0 * rho - 19.0 * sq)
    n2 = 12.0 * f[0] - 4.0 * axes + edges - (3.0 * rho - 5.5 * sq)
    a9 = 2.0 * s1 - s23
    b9 = exx - 2.0 * eyz
    q9 = 3.0 * xx - sq
    b11 = exy - exz
    q11 = yy - zz
    t1 = n1 * (1.19 / 2394.0)
    t2 = n2 * (1.4 / 252.0)
    t4 = (gx - 4.0 * d1 + (2.0 / 3.0) * jx) * (1.2 / 40.0)
    t6 = (gy - 4.0 * d2 + (2.0 / 3.0) * jy) * (1.2 / 40.0)
    t8 = (gz - 4.0 * d3 + (2.0 / 3.0) * jz) * (1.2 / 40.0)
    t9 = (a9 + b9 - q9) * (shear * (1.0 / 36.0))
    t10 = (b9 - 2.0 * a9 + 0.5 * q9) * (1.4 / 72.0)
    t11 = (m23 + b11 - q11) * (shear * (1.0 / 12.0))
    t12 = (b11 - 2.0 * m23 + 0.5 * q11) * (1.4 / 24.0)
    quarter = shear * 0.25
    t13 = (e1 - e2 - jx * uy) * quarter
    t14 = (e5 - e6 - jy * uz) * quarter
    t15 = (e3 - e4 - jx * uz) * quarter
    t16 = (gp - hp) * (1.98 / 8.0)
    t17 = (kp - gm) * (1.98 / 8.0)
    t18 = (hm - km) * (1.98 / 8.0)
    axis = -11.0 * t1 - 4.0 * t2
    edge = 8.0 * t1 + t2
    p9 = t9 - 2.0 * t10
    p11 = t11 - 2.0 * t12
    r9 = t9 + t10
    r11 = t11 + t12
    out = [None] * 19
    out[0] = f[0] + 30.0 * t1 - 12.0 * t2

    def put(i, even, odd):
        out[i] = f[i] - (even + odd)
        out[i + 1] = f[i + 1] - (even - odd)

    put(1, axis + 2.0 * p9, -4.0 * t4)
    put(3, axis - p9 + p11, -4.0 * t6)
    put(5, axis - p9 - p11, -4.0 * t8)
    vxy, vxz, vyz = edge + r9 + r11, edge + r9 - r11, edge - 2.0 * r9
    put(7, vxy + t13, t4 + t6 + (t16 - t17))
    put(9, vxy - t13, t4 - t6 + (t16 + t17))
    put(11, vxz + t15, t4 + t8 - (t16 - t18))
    put(13, vxz - t15, t4 - t8 - (t16 + t18))
    put(15, vyz + t14, t6 + t8 + (t17 - t18))
    put(17, vyz - t14, t6 - t8 + (t17 + t18))
    return out


def collide_kernel(par, pops_hbm, shear_hbm, post, near, far, pops, sems):
    even = par[0] == 0
    rate_copy = pltpu.make_async_copy(shear_hbm, post.at[SHEAR], sems.at[4])
    rate_copy.start()
    copies = []
    for plane in range(2):
        for half in range(2):
            rows = slice(8 * half, 8 * half + 8)
            copy = pltpu.make_async_copy(
                pops_hbm.at[:, plane, rows, :], pops.at[:, plane, rows, :], sems.at[2 * plane + half]
            )
            copy.start()
            copies.append(copy)
    rate_copy.wait()
    for plane in range(2):
        for half in range(2):
            rows = slice(8 * half, 8 * half + 8)
            copies[2 * plane + half].wait()
            rate = post[SHEAR, plane, rows, :]
            out = relax([pops[i, plane, rows, :] for i in range(19)], rate)
            for i in range(19):
                post[i, plane, rows, :] = out[i]

    for slot in range(20):
        up = post[X_LOW[slot][0], X_LOW[slot][1] + 2]
        down = post[X_HIGH[slot][0], X_HIGH[slot][1] - 2]
        near[slot] = jnp.where(even, up, down)
        far[slot] = jnp.where(even, down, up)


def reader(par, post, near, far):
    even = par[0] == 0

    def main(q, rows=slice(0, 16)):
        if q < 20:
            return jnp.where(even, far[q, rows, :], near[q, rows, :])
        if q >= 60:
            return jnp.where(even, near[q - 60, rows, :], far[q - 60, rows, :])
        field, plane = PAIRS[q]
        return post[field, plane, rows, :]

    return main


def z_pack_kernel(par, post, xnear, xfar, edge, near, far):
    main = reader(par, post, xnear, xfar)
    even = par[2] == 0
    lane = lax.broadcasted_iota(jnp.int32, (16, 128), 1)
    for tile in range(2):
        high = jnp.zeros((16, 128), jnp.float32)
        low = jnp.zeros((16, 128), jnp.float32)
        for slot in range(FIRST if tile == 0 else len(PAIRS) - FIRST):
            value = main(tile * FIRST + slot)
            mine = (lane >= 3 * slot) & (lane < 3 * slot + 3)
            high = jnp.where(mine, pltpu.roll(value, (3 * slot + 3) % 128, 1), high)
            low = jnp.where(mine, pltpu.roll(value, 3 * slot, 1), low)
        if tile == 1:
            sums = edge[...] + pltpu.roll(edge[...], 112, 1)
            odd = jnp.bitwise_and(lane - DEP_LANE, 1) == 1
            ours = (lane >= DEP_LANE) & (lane < DEP_LANE + 8)
            for shift in (DEP_LANE, DEP_LANE - 8):
                placed = pltpu.roll(sums, shift, 1)
                placed = jnp.where(odd, placed[16:32, :], placed[0:16, :])
                if shift == DEP_LANE:
                    high = jnp.where(ours, placed, high)
                else:
                    low = jnp.where(ours, placed, low)
        near[tile] = jnp.where(even, high, low)
        far[tile] = jnp.where(even, low, high)


def y_pack_kernel(par, post, xnear, xfar, znear, zfar, edge, near, far):
    main = reader(par, post, xnear, xfar)
    even = par[1] == 0
    even_z = par[2] == 0

    def put(row, count, high, low):
        near[row : row + count, :] = jnp.where(even, high, low)
        far[row : row + count, :] = jnp.where(even, low, high)

    top, bottom = slice(13, 16), slice(0, 3)
    for q in range(len(PAIRS)):
        put(3 * q, 3, main(q, top), main(q, bottom))
    put(240, 8, edge[0:8, :], edge[8:16, :])
    for tile in range(2):
        put(
            248 + 3 * tile,
            3,
            jnp.where(even_z, zfar[tile, top, :], znear[tile, top, :]),
            jnp.where(even_z, zfar[tile, bottom, :], znear[tile, bottom, :]),
        )
        put(
            254 + 3 * tile,
            3,
            jnp.where(even_z, znear[tile, top, :], zfar[tile, top, :]),
            jnp.where(even_z, znear[tile, bottom, :], zfar[tile, bottom, :]),
        )
    near[260:264, :] = jnp.zeros((4, 128), jnp.float32)
    far[260:264, :] = jnp.zeros((4, 128), jnp.float32)


def shifted(value, shift_y, shift_z):
    if shift_y:
        value = pltpu.roll(value, shift_y % 24, 0)
    if shift_z:
        value = pltpu.roll(value, shift_z % 256, 1)
    return value


def step_kernel(
    par,
    post,
    xnear,
    xfar,
    znear,
    zfar,
    ynear,
    yfar,
    dep_a,
    dep_b,
    pops_out,
    fluid,
    partial,
    snear,
    sfar,
    columns,
    field_ext,
    second,
):
    main = reader(par, post, xnear, xfar)
    even_x, even_y, even_z = par[0] == 0, par[1] == 0, par[2] == 0

    def dep(c, k, plane):
        return (dep_a if c < 2 else dep_b)[c % 2, k, plane]

    def y_low(row, count):
        return jnp.where(even_y, yfar[row : row + count, :], ynear[row : row + count, :])

    def y_high(row, count):
        return jnp.where(even_y, ynear[row : row + count, :], yfar[row : row + count, :])

    zero = jnp.zeros((8, 128), jnp.float32)
    for tile in range(2):
        for side in range(2):
            a, b = (zfar, znear) if side == 0 else (znear, zfar)
            columns[side, tile, 0:16, :] = jnp.where(even_z, a[tile], b[tile])
            columns[side, tile, 16:24, :] = zero
            row = 248 + 6 * side + 3 * tile
            columns[side, tile, 16:19, :] = y_high(row, 3)
            columns[side, tile, 21:24, :] = y_low(row, 3)
    lane = lax.broadcasted_iota(jnp.int32, (24, 128), 1)
    for q in range(len(PAIRS)):
        tile, slot = (0, q) if q < FIRST else (1, q - FIRST)
        field_ext[q, 0:16, 0:128] = main(q)
        field_ext[q, 16:24, 0:128] = zero
        field_ext[q, 16:19, 0:128] = y_high(3 * q, 3)
        field_ext[q, 21:24, 0:128] = y_low(3 * q, 3)
        low = pltpu.roll(columns[0, tile], (125 - 3 * slot) % 128, 1)
        high = pltpu.roll(columns[1, tile], (-3 * slot) % 128, 1)
        field_ext[q, :, 128:256] = jnp.where(lane < 64, high, low)

    for plane in range(4):
        for i in range(19):
            cx, cy, cz = SPEEDS[i]
            value = field_ext[INDEX[(i, plane - 1 - cx)]]
            second[i, plane] = shifted(value, cy, cz).reshape(3, 8, 256)

    for plane in range(4):
        rates = INDEX[(SHEAR, plane - 1)]

        def body(t, carry, plane=plane, rates=rates):
            row = pl.multiple_of(t * 8, 8)
            for z in range(2):
                lanes = slice(128 * z, 128 * z + 128)
                rate = field_ext[rates, pl.ds(row, 8), lanes]
                out = relax([second[i, plane, t, :, lanes] for i in range(19)], rate)
                for i in range(19):
                    second[i, plane, t, :, lanes] = out[i]
            return carry

        lax.fori_loop(0, 3, body, 0)

    lane16 = lax.broadcasted_iota(jnp.int32, (16, 128), 1)
    row8 = lax.broadcasted_iota(jnp.int32, (8, 128), 0)
    totals = [[None, None] for _ in range(4)]
    ups, downs = [None] * 4, [None] * 4
    for plane in range(2):
        rho = jx = jy = jz = None

        def add(total, value, sign):
            if sign == 0:
                return total
            if total is None:
                return value if sign > 0 else -value
            return total + value if sign > 0 else total - value

        for i in range(19):
            cx, cy, cz = SPEEDS[i]
            value = shifted(second[i, plane + 1 - cx].reshape(24, 256), cy, cz)
            pops_out[i, plane] = value[0:16, 0:128]
            rho = add(rho, value, 1)
            jx, jy, jz = add(jx, value, cx), add(jy, value, cy), add(jz, value, cz)
        u = [jx / rho, jy / rho, jz / rho]
        for c in range(3):
            fluid[c, plane] = u[c][0:16, 0:128]

        def moved(k, speed):
            s = dep(3, k, plane)
            return [dep(c, k, plane) - speed[c] * s for c in range(3)] + [2.0 * s]

        inner = [u[c][0:16, 0:128] for c in range(3)]
        total = moved(0, inner)
        tops = moved(1, inner)
        bottoms = moved(2, inner)

        def y_ext(k):
            ghosts = []
            for c in range(4):
                row = 240 + 2 * c + plane
                if k == 3:
                    ghost = jnp.where(row8 == 7, jnp.broadcast_to(y_low(row, 1), (8, 128)), 0.0)
                else:
                    ghost = jnp.where(row8 == 0, jnp.broadcast_to(y_high(row, 1), (8, 128)), 0.0)
                ghosts.append(jnp.concatenate([dep(c, k, plane), ghost], 0))
            return ghosts

        def z_ext(k):
            ghosts = []
            for c in range(4):
                spot = DEP_LANE + 2 * c + plane
                if k == 5:
                    ghost = pltpu.roll(columns[0, 1, 0:16, :], (127 - spot) % 128, 1)
                    ghost = jnp.where(lane16 == 127, ghost, 0.0)
                else:
                    ghost = pltpu.roll(columns[1, 1, 0:16, :], (-spot) % 128, 1)
                    ghost = jnp.where(lane16 == 0, ghost, 0.0)
                ghosts.append(jnp.concatenate([dep(c, k, plane), ghost], 1))
            return ghosts

        for k, shift in ((3, 1), (4, 23)):
            v = y_ext(k)
            rows = [v[c] - jnp.where(v[3] != 0.0, u[c][:, 0:128] * v[3], 0.0) for c in range(3)]
            rows.append(2.0 * v[3])
            for c in range(4):
                total[c] = total[c] + pltpu.roll(rows[c], shift, 0)[0:16, :]
        for k, shift in ((5, 1), (6, 255)):
            v = z_ext(k)
            rows = [v[c] - jnp.where(v[3] != 0.0, u[c][0:16, :] * v[3], 0.0) for c in range(3)]
            rows.append(2.0 * v[3])
            for c in range(4):
                total[c] = total[c] + pltpu.roll(rows[c], shift, 1)[:, 0:128]
        for c in range(4):
            totals[c][plane] = total[c]
        if plane == 0:
            downs, held = bottoms, tops
        else:
            ups = tops
            for c in range(4):
                totals[c][0] = totals[c][0] + bottoms[c]
                totals[c][1] = totals[c][1] + held[c]
    for c in range(4):
        partial[c, 0] = totals[c][0]
        partial[c, 1] = totals[c][1]
        snear[c] = jnp.where(even_x, ups[c], downs[c])
        sfar[c] = jnp.where(even_x, downs[c], ups[c])


def pieces(value):
    coarse = value.astype(jnp.bfloat16)
    return coarse, (value - coarse.astype(jnp.float32)).astype(jnp.bfloat16)


def small(value):
    return value.astype(jnp.float32).astype(jnp.bfloat16)


def numbers(rows, width):
    return lax.broadcasted_iota(jnp.int32, (rows, width), 0)


BY_LANE = (((1,), (1,)), ((), ()))


def deposit_kernel(fields, cell, move, mask, mass, velocity, out, picked, keys):
    where = cell[...]
    width = where.shape[1]
    code = small(move[...] * 32 + jnp.right_shift(where, 7))
    spot = small(jnp.bitwise_and(where, 127))
    weight = 0.5 * mask[...].astype(jnp.float32) * mass[...]
    rows = small(numbers(256, width))
    keys[...] = jnp.where(rows == code, jnp.bfloat16(1), jnp.bfloat16(0))
    here = rows[0:128] == spot
    for n, c in enumerate(fields):
        value = weight * velocity[c : c + 1, :] if c < 3 else weight
        for piece, part in enumerate(pieces(value)):
            at = 256 * n + 128 * piece
            picked[at : at + 128, :] = jnp.where(here, part, jnp.bfloat16(0))
    total = lax.dot_general(
        keys[...], picked[...], BY_LANE, preferred_element_type=jnp.float32
    )
    for n in range(2):
        out[n] = total[:, 256 * n : 256 * n + 128] + total[:, 256 * n + 128 : 256 * n + 256]


def edge_rows(mask, mass, velocity, target, code):
    weight = 0.5 * mask[...].astype(jnp.float32) * mass[...]
    width = weight.shape[1]
    values = [weight * velocity[c : c + 1, :] for c in range(3)] + [weight]
    field = jnp.bitwise_and(jnp.right_shift(numbers(16, width), 1), 3)
    chosen = jnp.where(field == 0, values[0], values[1])
    chosen = jnp.where(field == 2, values[2], chosen)
    chosen = jnp.where(field == 3, values[3], chosen)
    chosen = jnp.where(code == target, chosen, 0.0)
    return jnp.concatenate(pieces(chosen), 0)


def z_edge_kernel(cell, move, mask, mass, velocity, out):
    where = cell[...]
    width = where.shape[1]
    low = jnp.right_shift(numbers(16, width), 3)
    target = jnp.where(low == 0, 5 * 128 + 127, 6 * 128)
    code = move[...] * 128 + jnp.bitwise_and(where, 127)
    rows = edge_rows(mask, mass, velocity, target, code)
    line = jnp.where(
        small(numbers(32, width)) == small(jnp.right_shift(where, 7)), jnp.bfloat16(1), jnp.bfloat16(0)
    )
    out[...] = jnp.zeros_like(out)
    out[:, 0:32] = lax.dot_general(line, rows, BY_LANE, preferred_element_type=jnp.float32)


def y_edge_kernel(cell, move, mask, mass, velocity, out, tall):
    where = cell[...]
    width = where.shape[1]
    row = numbers(16, width)
    plane = jnp.bitwise_and(row, 1) * 16
    target = jnp.where(row < 8, 3 * 32 + 15 + plane, 4 * 32 + plane)
    code = move[...] * 32 + jnp.right_shift(where, 7)
    rows = edge_rows(mask, mass, velocity, target, code)
    here = jnp.where(
        small(numbers(128, width)) == small(jnp.bitwise_and(where, 127)), jnp.bfloat16(1), jnp.bfloat16(0)
    )
    total = lax.dot_general(rows, here, BY_LANE, preferred_element_type=jnp.float32)
    out[...] = total[0:16, :] + total[16:32, :]
    for j in range(width // 128):
        for c in range(3):
            tall[c, j : j + 1, :] = velocity[c : c + 1, 128 * j : 128 * j + 128]


def drag_kernel(cell, mask, velocity, fluid, out):
    for group in range(8):
        rows = slice(8 * group, 8 * group + 8)
        where = cell[rows, :]
        lane = jnp.bitwise_and(where, 127)
        line = jnp.right_shift(where, 7)
        picked = [jnp.zeros((8, 128), jnp.float32) for _ in range(3)]
        for r in range(32):
            mine = line == r
            for c in range(3):
                table = jnp.broadcast_to(fluid[c, r : r + 1, :], (8, 128))
                value = jnp.take_along_axis(table, lane, axis=1)
                picked[c] = jnp.where(mine, value, picked[c])
        half = 0.5 * mask[rows, :].astype(jnp.float32)
        for c in range(3):
            old = velocity[c, rows, :]
            new = old + half * (picked[c] - old)
            for r in range(8):
                at = 128 * (8 * group + r)
                out[c : c + 1, at : at + 128] = new[r : r + 1, :]


def swap(value, axis, shifted_by_one):
    count = lax.axis_size(axis)
    pairs = []
    for i in range(count):
        if shifted_by_one:
            pairs.append((i, (i + 1) % count if i % 2 else (i - 1) % count))
        else:
            pairs.append((i, i ^ 1))
    return lax.ppermute(value, axis, pairs)


def both_swaps(near, far, axis):
    far = swap(far, axis, True)
    near = swap(near, axis, False)
    return near, far


def struct(*shape):
    return jax.ShapeDtypeStruct(shape, jnp.float32)


def call(kernel, outs, args, specs=None, scratch=(), flops=1000000, size=1000000):
    single = not isinstance(outs, tuple)
    return pl.pallas_call(
        kernel,
        out_shape=outs,
        in_specs=specs or [VMEM] * len(args),
        out_specs=VMEM if single else (VMEM,) * len(outs),
        scratch_shapes=scratch,
        compiler_params=pltpu.CompilerParams(vmem_limit_bytes=40 << 20),
        cost_estimate=pl.CostEstimate(flops=flops, bytes_accessed=size, transcendentals=0),
    )(*args)


def body(populations, shear_rate, part_cell, part_move, part_mask, part_velocity, part_mass):
    par = jnp.stack([lax.axis_index(a) % 2 for a in ("gx", "gy", "gz")]).astype(jnp.int32)
    count = part_cell.shape[0]
    flat = (1, count)
    particles = (
        part_cell.reshape(flat),
        part_move.reshape(flat),
        part_mask.reshape(flat),
        part_mass.reshape(flat),
        part_velocity,
    )

    post, near, far = call(
        collide_kernel,
        (struct(20, 2, 16, 128), struct(20, 16, 128), struct(20, 16, 128)),
        (
            par,
            pltpu.with_memory_space_constraint(populations, pltpu.HBM),
            pltpu.with_memory_space_constraint(shear_rate, pltpu.HBM),
        ),
        [SMEM, HBM, HBM],
        [pltpu.VMEM((19, 2, 16, 128), jnp.float32), pltpu.SemaphoreType.DMA((5,))],
    )
    xnear, xfar = both_swaps(near, far, "gx")

    edge = call(z_edge_kernel, struct(32, 128), particles)
    near, far = call(
        z_pack_kernel,
        (struct(2, 16, 128), struct(2, 16, 128)),
        (par, post, xnear, xfar, edge),
        [SMEM] + [VMEM] * 4,
    )
    znear, zfar = both_swaps(near, far, "gz")

    edge, velocity_tall = call(
        y_edge_kernel, (struct(16, 128), struct(3, count // 128, 128)), particles
    )
    scratch = [pltpu.VMEM((512, count), jnp.bfloat16), pltpu.VMEM((256, count), jnp.bfloat16)]
    deposits = [
        call(
            functools.partial(deposit_kernel, fields),
            struct(2, 256, 128),
            particles,
            scratch=scratch,
            flops=2000000000,
        ).reshape(2, 8, 2, 16, 128)
        for fields in ((0, 1), (2, 3))
    ]
    near, far = call(
        y_pack_kernel,
        (struct(Y_ROWS, 128), struct(Y_ROWS, 128)),
        (par, post, xnear, xfar, znear, zfar, edge),
        [SMEM] + [VMEM] * 6,
    )
    ynear, yfar = both_swaps(near, far, "gy")

    populations_out, fluid, partial, near, far = call(
        step_kernel,
        (
            struct(19, 2, 16, 128),
            struct(3, 2, 16, 128),
            struct(4, 2, 16, 128),
            struct(4, 16, 128),
            struct(4, 16, 128),
        ),
        (par, post, xnear, xfar, znear, zfar, ynear, yfar, *deposits),
        [SMEM] + [VMEM] * 9,
        [
            pltpu.VMEM((2, 2, 24, 128), jnp.float32),
            pltpu.VMEM((len(PAIRS), 24, 256), jnp.float32),
            pltpu.VMEM((19, 4, 3, 8, 256), jnp.float32),
        ],
        flops=20000000,
    )
    snear, sfar = both_swaps(near, far, "gx")

    tall = (count // 128, 128)
    velocity_out = call(
        drag_kernel,
        struct(3, count),
        (
            part_cell.reshape(tall),
            part_mask.reshape(tall),
            velocity_tall,
            fluid.reshape(3, 32, 128),
        ),
    )

    even = par[0] == 0
    upper = lax.broadcasted_iota(jnp.int32, partial.shape, 1) == 1
    sources = partial + jnp.where(upper == even, snear[:, None], sfar[:, None])
    return populations_out, sources, velocity_out


def solution(mesh):
    placed = (
        P(None, "gx", "gy", "gz"),
        P("gx", "gy", "gz"),
        P(("gx", "gy", "gz")),
        P(("gx", "gy", "gz")),
        P(("gx", "gy", "gz")),
        P(None, ("gx", "gy", "gz")),
        P(("gx", "gy", "gz")),
    )
    return jax.shard_map(
        body,
        mesh=mesh,
        in_specs=placed,
        out_specs=(
            P(None, "gx", "gy", "gz"),
            P(None, "gx", "gy", "gz"),
            P(None, ("gx", "gy", "gz")),
        ),
        check_vma=False,
    )
```

profile of v0, /device:TPU:6, one launch (start us, length us, event | category | flops | bytes accessed | tf_op | source)
XLA Modules:
  0.0 74.3 jit_solution(2869656940903989342)
XLA Ops:
  0.7 0.1 pad_add_fusion.par
  0.7 0.0 copy-start.4
  0.8 1.7 %shard_map.94 = (f32[20,2,16,128]{3,2,1,0:T(8,128)S(1)}, f32[20,16,128]{2,1,0:T(8,128)S(1)}, f32[20,16,128]{2,1,0:T(8,128)S(1)}) custom-call(s32[3]{0:T(128)S(1)} %pad_add_fusion.par, f32[19,2,16,128]{3,2,1,0:T(8,128)} %pops_hbm.1, f32[2,16,128]{2,1,0:T(8,128)} %shear_hbm.1), custom_call_target="tpu_custom_call" | custom-call | flops 1000000 | bytes 1000000 | tf_op jit(solution)/shard_map/pallas_call | solution.py:511
  2.4 2.7 %collective-permute-start = (f32[20,16,128]{2,1,0:T(8,128)S(1)}, f32[20,16,128]{2,1,0:T(8,128)S(1)}, u32[]{:S(2)}, u32[]{:S(2)}) collective-permute-start(f32[20,16,128]{2,1,0:T(8,128)S(1)} %get-tuple-element.18), channel_id=1, source_target_pairs={{0,256},{256,0},{512,768},{768,512},{1,257},{257,1},{513,769},{769... | collective-permute-start | bytes 491528 | tf_op jit(solution)/shard_map/ppermute | solution.py:496
  5.2 14.2 %collective-permute-start.1 = (f32[20,16,128]{2,1,0:T(8,128)S(1)}, f32[20,16,128]{2,1,0:T(8,128)S(1)}, u32[]{:S(2)}, u32[]{:S(2)}) collective-permute-start(f32[20,16,128]{2,1,0:T(8,128)S(1)} %get-tuple-element.19), channel_id=1, source_target_pairs={{0,768},{256,512},{512,256},{768,0},{1,769},{257,513},{513,257},{7... | collective-permute-start | bytes 491528 | tf_op jit(solution)/shard_map/ppermute | solution.py:496
  19.4 0.0 copy-done
  19.4 0.0 copy-done.1
  19.4 0.0 copy-done.2
  19.4 0.0 copy-done.3
  19.4 0.4 shard_map.95.edge
  19.8 0.0 collective-permute-done.xnear
  19.8 2.8 %collective-permute-done.1.xfar = f32[20,16,128]{2,1,0:T(8,128)S(1)} collective-permute-done((f32[20,16,128]{2,1,0:T(8,128)S(1)}, f32[20,16,128]{2,1,0:T(8,128)S(1)}, u32[]{:S(2)}, u32[]{:S(2)}) %collective-permute-start.1) | collective-permute-done | bytes 163872 | tf_op jit(solution)/shard_map/ppermute | solution.py:496
  22.7 1.0 %shard_map.96 = (f32[2,16,128]{2,1,0:T(8,128)S(1)}, f32[2,16,128]{2,1,0:T(8,128)S(1)}) custom-call(s32[3]{0:T(128)S(1)} %pad_add_fusion.par, f32[20,2,16,128]{3,2,1,0:T(8,128)S(1)} %get-tuple-element.17.post, f32[20,16,128]{2,1,0:T(8,128)S(1)} %collective-permute-done.xnear, f32[20,16,128]{2,1,0:T(8,128)S(1)} %collective-permute-done.1.xfar, ...), custom_call_target="tpu_custom_call" | custom-call | flops 1000000 | bytes 1000000 | tf_op jit(solution)/shard_map/pallas_call | solution.py:511
  23.7 1.9 %collective-permute-start.2 = (f32[2,16,128]{2,1,0:T(8,128)S(1)}, f32[2,16,128]{2,1,0:T(8,128)S(1)}, u32[]{:S(2)}, u32[]{:S(2)}) collective-permute-start(f32[2,16,128]{2,1,0:T(8,128)S(1)} %get-tuple-element.20), channel_id=1, source_target_pairs={{0,1},{1,0},{2,3},{3,2},{4,5},{5,4},{6,7},{7,6},{8,9},{9,8},{10,11... | collective-permute-start | bytes 49160 | tf_op jit(solution)/shard_map/ppermute | solution.py:496
  25.6 7.7 %collective-permute-start.3 = (f32[2,16,128]{2,1,0:T(8,128)S(1)}, f32[2,16,128]{2,1,0:T(8,128)S(1)}, u32[]{:S(2)}, u32[]{:S(2)}) collective-permute-start(f32[2,16,128]{2,1,0:T(8,128)S(1)} %get-tuple-element.21), channel_id=1, source_target_pairs={{0,15},{1,2},{2,1},{3,4},{4,3},{5,6},{6,5},{7,8},{8,7},{9,10},{10,... | collective-permute-start | bytes 49160 | tf_op jit(solution)/shard_map/ppermute | solution.py:496
  33.3 2.4 %shard_map.100 = f32[2,256,128]{2,1,0:T(8,128)S(1)} custom-call(s32[1,8192]{1,0:T(1,128)S(1)} %bitcast.13, s32[1,8192]{1,0:T(1,128)S(1)} %bitcast.25, s32[1,8192]{1,0:T(1,128)S(1)} %bitcast.18, f32[1,8192]{1,0:T(1,128)S(1)} %bitcast.29, f32[3,8192]{1,0:T(4,128)S(1)} %copy-done), custom_call_target="tpu_custom_call" | custom-call | flops 2000000000 | bytes 1000000 | tf_op jit(solution)/shard_map/pallas_call | solution.py:511
  35.7 0.8 %shard_map.97 = (f32[16,128]{1,0:T(8,128)S(1)}, f32[3,64,128]{2,1,0:T(8,128)S(1)}) custom-call(s32[1,8192]{1,0:T(1,128)S(1)} %bitcast.14, s32[1,8192]{1,0:T(1,128)S(1)} %bitcast.26, s32[1,8192]{1,0:T(1,128)S(1)} %bitcast.19, f32[1,8192]{1,0:T(1,128)S(1)} %bitcast.30, f32[3,8192]{1,0:T(4,128)S(1)} %copy-done), custom_call_target="tpu_custom_call" | custom-call | flops 1000000 | bytes 1000000 | tf_op jit(solution)/shard_map/pallas_call | solution.py:511
  36.5 0.0 collective-permute-done.2.znear
  36.5 0.8 %collective-permute-done.3.zfar = f32[2,16,128]{2,1,0:T(8,128)S(1)} collective-permute-done((f32[2,16,128]{2,1,0:T(8,128)S(1)}, f32[2,16,128]{2,1,0:T(8,128)S(1)}, u32[]{:S(2)}, u32[]{:S(2)}) %collective-permute-start.3) | collective-permute-done | bytes 16416 | tf_op jit(solution)/shard_map/ppermute | solution.py:496
  37.2 0.6 shard_map.98
  37.9 2.7 %collective-permute-start.4 = (f32[264,128]{1,0:T(8,128)S(1)}, f32[264,128]{1,0:T(8,128)S(1)}, u32[]{:S(2)}, u32[]{:S(2)}) collective-permute-start(f32[264,128]{1,0:T(8,128)S(1)} %get-tuple-element.23), channel_id=1, source_target_pairs={{0,16},{16,0},{32,48},{48,32},{64,80},{80,64},{96,112},{112,96},{1... | collective-permute-start | bytes 405512 | tf_op jit(solution)/shard_map/ppermute | solution.py:496
  40.6 14.5 %collective-permute-start.5 = (f32[264,128]{1,0:T(8,128)S(1)}, f32[264,128]{1,0:T(8,128)S(1)}, u32[]{:S(2)}, u32[]{:S(2)}) collective-permute-start(f32[264,128]{1,0:T(8,128)S(1)} %get-tuple-element.24), channel_id=1, source_target_pairs={{0,240},{16,32},{32,16},{48,64},{64,48},{80,96},{96,80},{112,128},... | collective-permute-start | bytes 405512 | tf_op jit(solution)/shard_map/ppermute | solution.py:496
  55.1 2.4 %shard_map.99 = f32[2,256,128]{2,1,0:T(8,128)S(1)} custom-call(s32[1,8192]{1,0:T(1,128)S(1)} %bitcast.15, s32[1,8192]{1,0:T(1,128)S(1)} %bitcast.27, s32[1,8192]{1,0:T(1,128)S(1)} %bitcast.20, f32[1,8192]{1,0:T(1,128)S(1)} %bitcast.31, f32[3,8192]{1,0:T(4,128)S(1)} %copy-done), custom_call_target="tpu_custom_call" | custom-call | flops 2000000000 | bytes 1000000 | tf_op jit(solution)/shard_map/pallas_call | solution.py:511
  57.5 0.0 collective-permute-done.4.ynear
  57.5 2.1 %collective-permute-done.5.yfar = f32[264,128]{1,0:T(8,128)S(1)} collective-permute-done((f32[264,128]{1,0:T(8,128)S(1)}, f32[264,128]{1,0:T(8,128)S(1)}, u32[]{:S(2)}, u32[]{:S(2)}) %collective-permute-start.5) | collective-permute-done | bytes 135200 | tf_op jit(solution)/shard_map/ppermute | solution.py:496
  59.6 3.4 %shard_map.101 = (f32[19,2,16,128]{3,2,1,0:T(8,128)}, f32[3,2,16,128]{3,2,1,0:T(8,128)S(1)}, f32[4,2,16,128]{3,2,1,0:T(8,128)S(1)}, f32[4,16,128]{2,1,0:T(8,128)S(1)}, f32[4,16,128]{2,1,0:T(8,128)S(1)}) custom-call(s32[3]{0:T(128)S(1)} %pad_add_fusion.par, f32[20,2,16,128]{3,2,1,0:T(8,128)S(1)} %get-tuple-element.17.post, ...), custom_call_target="tpu_custom_call" | custom-call | flops 20000000 | bytes 1000000 | tf_op jit(solution)/shard_map/pallas_call | solution.py:511
  63.0 3.2 %collective-permute-start.6 = (f32[4,16,128]{2,1,0:T(8,128)S(1)}, f32[4,16,128]{2,1,0:T(8,128)S(1)}, u32[]{:S(2)}, u32[]{:S(2)}) collective-permute-start(f32[4,16,128]{2,1,0:T(8,128)S(1)} %get-tuple-element.27), channel_id=1, source_target_pairs={{0,256},{256,0},{512,768},{768,512},{1,257},{257,1},{513,769},{769... | collective-permute-start | bytes 98312 | tf_op jit(solution)/shard_map/ppermute | solution.py:496
  66.2 5.5 %collective-permute-start.7 = (f32[4,16,128]{2,1,0:T(8,128)S(1)}, f32[4,16,128]{2,1,0:T(8,128)S(1)}, u32[]{:S(2)}, u32[]{:S(2)}) collective-permute-start(f32[4,16,128]{2,1,0:T(8,128)S(1)} %get-tuple-element.28), channel_id=1, source_target_pairs={{0,768},{256,512},{512,256},{768,0},{1,769},{257,513},{513,257},{7... | collective-permute-start | bytes 98312 | tf_op jit(solution)/shard_map/ppermute | solution.py:496
  71.8 1.6 %shard_map.102 = f32[3,8192]{1,0:T(4,128)} custom-call(s32[64,128]{1,0:T(8,128)S(1)} %bitcast.16, s32[64,128]{1,0:T(8,128)S(1)} %bitcast.21, f32[3,64,128]{2,1,0:T(8,128)S(1)} %get-tuple-element.29.velocity, f32[3,32,128]{2,1,0:T(8,128)S(1)} %bitcast.32), custom_call_target="tpu_custom_call" | custom-call | flops 1000000 | bytes 1000000 | tf_op jit(solution)/shard_map/pallas_call | solution.py:511
  73.3 0.0 collective-permute-done.6
  73.3 0.3 collective-permute-done.7
  73.6 0.7 select_add_fusion
  (6 shorter events, 0.0 us)
Async XLA Ops:
  0.7 18.7 %copy-start = (f32[3,8192]{1,0:T(4,128)S(1)}, f32[3,8192]{1,0:T(4,128)}, u32[]{:S(2)}) copy-start(f32[3,8192]{1,0:T(4,128)} %velocity.7) | copy-start | bytes 294916
  0.7 18.7 %copy-start.1 = (s32[8192]{0:T(1024)S(1)}, s32[8192]{0:T(1024)}, u32[]{:S(2)}) copy-start(s32[8192]{0:T(1024)} %param.9) | copy-start | bytes 98308
  0.7 18.7 %copy-start.2 = (s32[8192]{0:T(1024)S(1)}, s32[8192]{0:T(1024)}, u32[]{:S(2)}) copy-start(s32[8192]{0:T(1024)} %param.11) | copy-start | bytes 98308
  0.7 18.7 %copy-start.3 = (s32[8192]{0:T(1024)S(1)}, s32[8192]{0:T(1024)}, u32[]{:S(2)}) copy-start(s32[8192]{0:T(1024)} %param.10) | copy-start | bytes 98308
  0.7 18.7 %copy-start.4 = (f32[8192]{0:T(1024)S(1)}, f32[8192]{0:T(1024)}, u32[]{:S(2)}) copy-start(f32[8192]{0:T(1024)} %param.13) | copy-start | bytes 98308
  2.4 17.4 %collective-permute-start = (f32[20,16,128]{2,1,0:T(8,128)S(1)}, f32[20,16,128]{2,1,0:T(8,128)S(1)}, u32[]{:S(2)}, u32[]{:S(2)}) collective-permute-start(f32[20,16,128]{2,1,0:T(8,128)S(1)} %get-tuple-element.18), channel_id=1, source_target_pairs={{0,256},{256,0},{512,768},{768,512},{1,257},{257,1},{513,769},{769... | collective-permute-start | bytes 491528 | tf_op jit(solution)/shard_map/ppermute | solution.py:496
  5.2 17.5 %collective-permute-start.1 = (f32[20,16,128]{2,1,0:T(8,128)S(1)}, f32[20,16,128]{2,1,0:T(8,128)S(1)}, u32[]{:S(2)}, u32[]{:S(2)}) collective-permute-start(f32[20,16,128]{2,1,0:T(8,128)S(1)} %get-tuple-element.19), channel_id=1, source_target_pairs={{0,768},{256,512},{512,256},{768,0},{1,769},{257,513},{513,257},{7... | collective-permute-start | bytes 491528 | tf_op jit(solution)/shard_map/ppermute | solution.py:496
  23.7 12.8 %collective-permute-start.2 = (f32[2,16,128]{2,1,0:T(8,128)S(1)}, f32[2,16,128]{2,1,0:T(8,128)S(1)}, u32[]{:S(2)}, u32[]{:S(2)}) collective-permute-start(f32[2,16,128]{2,1,0:T(8,128)S(1)} %get-tuple-element.20), channel_id=1, source_target_pairs={{0,1},{1,0},{2,3},{3,2},{4,5},{5,4},{6,7},{7,6},{8,9},{9,8},{10,11... | collective-permute-start | bytes 49160 | tf_op jit(solution)/shard_map/ppermute | solution.py:496
  25.6 11.7 %collective-permute-start.3 = (f32[2,16,128]{2,1,0:T(8,128)S(1)}, f32[2,16,128]{2,1,0:T(8,128)S(1)}, u32[]{:S(2)}, u32[]{:S(2)}) collective-permute-start(f32[2,16,128]{2,1,0:T(8,128)S(1)} %get-tuple-element.21), channel_id=1, source_target_pairs={{0,15},{1,2},{2,1},{3,4},{4,3},{5,6},{6,5},{7,8},{8,7},{9,10},{10,... | collective-permute-start | bytes 49160 | tf_op jit(solution)/shard_map/ppermute | solution.py:496
  37.9 19.7 %collective-permute-start.4 = (f32[264,128]{1,0:T(8,128)S(1)}, f32[264,128]{1,0:T(8,128)S(1)}, u32[]{:S(2)}, u32[]{:S(2)}) collective-permute-start(f32[264,128]{1,0:T(8,128)S(1)} %get-tuple-element.23), channel_id=1, source_target_pairs={{0,16},{16,0},{32,48},{48,32},{64,80},{80,64},{96,112},{112,96},{1... | collective-permute-start | bytes 405512 | tf_op jit(solution)/shard_map/ppermute | solution.py:496
  40.6 19.0 %collective-permute-start.5 = (f32[264,128]{1,0:T(8,128)S(1)}, f32[264,128]{1,0:T(8,128)S(1)}, u32[]{:S(2)}, u32[]{:S(2)}) collective-permute-start(f32[264,128]{1,0:T(8,128)S(1)} %get-tuple-element.24), channel_id=1, source_target_pairs={{0,240},{16,32},{32,16},{48,64},{64,48},{80,96},{96,80},{112,128},... | collective-permute-start | bytes 405512 | tf_op jit(solution)/shard_map/ppermute | solution.py:496
  63.0 10.3 %collective-permute-start.6 = (f32[4,16,128]{2,1,0:T(8,128)S(1)}, f32[4,16,128]{2,1,0:T(8,128)S(1)}, u32[]{:S(2)}, u32[]{:S(2)}) collective-permute-start(f32[4,16,128]{2,1,0:T(8,128)S(1)} %get-tuple-element.27), channel_id=1, source_target_pairs={{0,256},{256,0},{512,768},{768,512},{1,257},{257,1},{513,769},{769... | collective-permute-start | bytes 98312 | tf_op jit(solution)/shard_map/ppermute | solution.py:496
  66.2 7.4 %collective-permute-start.7 = (f32[4,16,128]{2,1,0:T(8,128)S(1)}, f32[4,16,128]{2,1,0:T(8,128)S(1)}, u32[]{:S(2)}, u32[]{:S(2)}) collective-permute-start(f32[4,16,128]{2,1,0:T(8,128)S(1)} %get-tuple-element.28), channel_id=1, source_target_pairs={{0,768},{256,512},{512,256},{768,0},{1,769},{257,513},{513,257},{7... | collective-permute-start | bytes 98312 | tf_op jit(solution)/shard_map/ppermute | solution.py:496
where the time goes:
time: 75.7 us; the launch traced here: 74.3 us
  starting transfers between devices  52.6 us (69%)
  Pallas kernels  14.2 us (19%)
  waiting for transfers between devices  5.95 us (8%)
  between operations  0.84 us (1%)
  other arithmetic  0.79 us (1%)
    ppermute x8, starting transfers between devices, swap(): return lax.ppermute(value, axis, pairs)  52.6 us
    pallas_call x9, Pallas kernels, call(): pl.pallas_call(kernel, out_shape=outs, in_specs=specs or [VMEM] * len(arg...  14.2 us
    ppermute x8, waiting for transfers between devices, swap(): return lax.ppermute(value, axis, pairs)  5.95 us
  transfers between devices with their start and end apart: 8, of which 4 were waited for; matrix products, arithmetic and copies ran while one was open for 0% of the time, Pallas kernels for 10%

commit v1 on v0

--- a/solution.py
+++ b/solution.py
@@ -115,7 +115,9 @@
     return out
 
 
-def collide_kernel(par, pops_hbm, shear_hbm, post, near, far, pops, sems):
+def collide_kernel(par, pops_hbm, shear_hbm, *refs):
+    given, (post, near, far), held = refs[0:5], refs[5:8], refs[8:13]
+    pops, sems = refs[13:]
     even = par[0] == 0
     rate_copy = pltpu.make_async_copy(shear_hbm, post.at[SHEAR], sems.at[4])
     rate_copy.start()
@@ -128,6 +130,10 @@
             )
             copy.start()
             copies.append(copy)
+    for n in range(5):
+        copy = pltpu.make_async_copy(given[n], held[n], sems.at[5 + n])
+        copy.start()
+        copies.append(copy)
     rate_copy.wait()
     for plane in range(2):
         for half in range(2):
@@ -143,6 +149,8 @@
         down = post[X_HIGH[slot][0], X_HIGH[slot][1] - 2]
         near[slot] = jnp.where(even, up, down)
         far[slot] = jnp.where(even, down, up)
+    for copy in copies[4:]:
+        copy.wait()
 
 
 def reader(par, post, near, far):
@@ -224,11 +232,59 @@
     return value
 
 
+def sided(first, second, tile):
+    tile, slot = tile
+    low = pltpu.roll(first[tile], (125 - 3 * slot) % 128, 1)
+    high = pltpu.roll(second[tile], (-3 * slot) % 128, 1)
+    lane = lax.broadcasted_iota(jnp.int32, low.shape, 1)
+    return jnp.where(lane < 64, high, low)
+
+
+def column_spot(q):
+    return (0, q) if q < FIRST else (1, q - FIRST)
+
+
+def collide_rows(rate_of, fields, plane, index):
+    for z in range(2):
+        lanes = slice(128 * z, 128 * z + 128)
+        at = index + (slice(None), lanes)
+        out = relax([fields[(i, plane) + at] for i in range(19)], rate_of(lanes))
+        for i in range(19):
+            fields[(i, plane) + at] = out[i]
+
+
+def inner_kernel(par, post, xnear, xfar, znear, zfar, field_ext, second):
+    main = reader(par, post, xnear, xfar)
+    even_z = par[2] == 0
+    low = [jnp.where(even_z, zfar[t], znear[t]) for t in range(2)]
+    high = [jnp.where(even_z, znear[t], zfar[t]) for t in range(2)]
+    for q in range(len(PAIRS)):
+        field_ext[q, :, 0:128] = main(q)
+        field_ext[q, :, 128:256] = sided(low, high, column_spot(q))
+    for plane in range(4):
+        for i in range(19):
+            cx, cy, cz = SPEEDS[i]
+            value = field_ext[INDEX[(i, plane - 1 - cx)]]
+            if cy:
+                value = pltpu.roll(value, cy % 16, 0)
+            if cz:
+                value = pltpu.roll(value, cz % 256, 1)
+            second[i, plane] = value.reshape(2, 8, 256)
+    for plane in range(4):
+        rates = INDEX[(SHEAR, plane - 1)]
+
+        def body(t, carry, plane=plane, rates=rates):
+            row = pl.multiple_of(t * 8, 8)
+            collide_rows(lambda lanes: field_ext[rates, pl.ds(row, 8), lanes], second, plane, (t,))
+            return carry
+
+        lax.fori_loop(0, 2, body, 0)
+
+
 def step_kernel(
     par,
-    post,
-    xnear,
-    xfar,
+    field_ext,
+    middle,
     znear,
     zfar,
     ynear,
@@ -240,11 +296,9 @@
     partial,
     snear,
     sfar,
-    columns,
-    field_ext,
-    second,
+    window,
+    rim,
 ):
-    main = reader(par, post, xnear, xfar)
     even_x, even_y, even_z = par[0] == 0, par[1] == 0, par[2] == 0
 
     def dep(c, k, plane):
@@ -256,46 +310,43 @@
     def y_high(row, count):
         return jnp.where(even_y, ynear[row : row + count, :], yfar[row : row + count, :])
 
-    zero = jnp.zeros((8, 128), jnp.float32)
-    for tile in range(2):
-        for side in range(2):
-            a, b = (zfar, znear) if side == 0 else (znear, zfar)
-            columns[side, tile, 0:16, :] = jnp.where(even_z, a[tile], b[tile])
-            columns[side, tile, 16:24, :] = zero
-            row = 248 + 6 * side + 3 * tile
-            columns[side, tile, 16:19, :] = y_high(row, 3)
-            columns[side, tile, 21:24, :] = y_low(row, 3)
-    lane = lax.broadcasted_iota(jnp.int32, (24, 128), 1)
+    pad = jnp.zeros((2, 128), jnp.float32)
+    packed = [
+        [
+            jnp.concatenate([y_high(row, 3), y_low(row, 3), pad], 0)
+            for row in (248 + 6 * side, 251 + 6 * side)
+        ]
+        for side in range(2)
+    ]
     for q in range(len(PAIRS)):
-        tile, slot = (0, q) if q < FIRST else (1, q - FIRST)
-        field_ext[q, 0:16, 0:128] = main(q)
-        field_ext[q, 16:24, 0:128] = zero
-        field_ext[q, 16:19, 0:128] = y_high(3 * q, 3)
-        field_ext[q, 21:24, 0:128] = y_low(3 * q, 3)
-        low = pltpu.roll(columns[0, tile], (125 - 3 * slot) % 128, 1)
-        high = pltpu.roll(columns[1, tile], (-3 * slot) % 128, 1)
-        field_ext[q, :, 128:256] = jnp.where(lane < 64, high, low)
+        window[q, 0:8, :] = field_ext[q, 8:16, :]
+        window[q, 8:11, 0:128] = y_high(3 * q, 3)
+        window[q, 11:14, 0:128] = y_low(3 * q, 3)
+        window[q, 8:14, 128:256] = sided(packed[0], packed[1], column_spot(q))[0:6, :]
+        window[q, 14:16, :] = field_ext[q, 0:2, :]
 
     for plane in range(4):
+        rates = INDEX[(SHEAR, plane - 1)]
         for i in range(19):
             cx, cy, cz = SPEEDS[i]
-            value = field_ext[INDEX[(i, plane - 1 - cx)]]
-            second[i, plane] = shifted(value, cy, cz).reshape(3, 8, 256)
-
-    for plane in range(4):
-        rates = INDEX[(SHEAR, plane - 1)]
-
-        def body(t, carry, plane=plane, rates=rates):
-            row = pl.multiple_of(t * 8, 8)
-            for z in range(2):
-                lanes = slice(128 * z, 128 * z + 128)
-                rate = field_ext[rates, pl.ds(row, 8), lanes]
-                out = relax([second[i, plane, t, :, lanes] for i in range(19)], rate)
-                for i in range(19):
-                    second[i, plane, t, :, lanes] = out[i]
-            return carry
-
-        lax.fori_loop(0, 3, body, 0)
+            value = window[INDEX[(i, plane - 1 - cx)], 7 - cy : 15 - cy, :]
+            if cz:
+                value = pltpu.roll(value, cz % 256, 1)
+            rim[i, plane] = value
+        collide_rows(lambda lanes, rates=rates: window[rates, 7:15, lanes], rim, plane, ())
+
+    row_of = lax.broadcasted_iota(jnp.int32, (8, 256), 0)
+
+    def collided(i, plane):
+        down, up = pltpu.roll(rim[i, plane], 1, 0), pltpu.roll(rim[i, plane], 7, 0)
+        return jnp.concatenate(
+            [
+                jnp.where(row_of == 0, down, middle[i, plane, 0]),
+                jnp.where(row_of == 7, up, middle[i, plane, 1]),
+                jnp.where(row_of < 4, up, down),
+            ],
+            0,
+        )
 
     lane16 = lax.broadcasted_iota(jnp.int32, (16, 128), 1)
     row8 = lax.broadcasted_iota(jnp.int32, (8, 128), 0)
@@ -313,7 +364,7 @@
 
         for i in range(19):
             cx, cy, cz = SPEEDS[i]
-            value = shifted(second[i, plane + 1 - cx].reshape(24, 256), cy, cz)
+            value = shifted(collided(i, plane + 1 - cx), cy, cz)
             pops_out[i, plane] = value[0:16, 0:128]
             rho = add(rho, value, 1)
             jx, jy, jz = add(jx, value, cx), add(jy, value, cy), add(jz, value, cz)
@@ -346,10 +397,12 @@
             for c in range(4):
                 spot = DEP_LANE + 2 * c + plane
                 if k == 5:
-                    ghost = pltpu.roll(columns[0, 1, 0:16, :], (127 - spot) % 128, 1)
+                    ghost = jnp.where(even_z, zfar[1], znear[1])
+                    ghost = pltpu.roll(ghost, (127 - spot) % 128, 1)
                     ghost = jnp.where(lane16 == 127, ghost, 0.0)
                 else:
-                    ghost = pltpu.roll(columns[1, 1, 0:16, :], (-spot) % 128, 1)
+                    ghost = jnp.where(even_z, znear[1], zfar[1])
+                    ghost = pltpu.roll(ghost, (-spot) % 128, 1)
                     ghost = jnp.where(lane16 == 0, ghost, 0.0)
                 ghosts.append(jnp.concatenate([dep(c, k, plane), ghost], 1))
             return ghosts
@@ -506,7 +559,7 @@
     return jax.ShapeDtypeStruct(shape, jnp.float32)
 
 
-def call(kernel, outs, args, specs=None, scratch=(), flops=1000000, size=1000000):
+def call(kernel, outs, args, specs=None, scratch=(), flops=1000000, vmem=40):
     single = not isinstance(outs, tuple)
     return pl.pallas_call(
         kernel,
@@ -514,8 +567,8 @@
         in_specs=specs or [VMEM] * len(args),
         out_specs=VMEM if single else (VMEM,) * len(outs),
         scratch_shapes=scratch,
-        compiler_params=pltpu.CompilerParams(vmem_limit_bytes=40 << 20),
-        cost_estimate=pl.CostEstimate(flops=flops, bytes_accessed=size, transcendentals=0),
+        compiler_params=pltpu.CompilerParams(vmem_limit_bytes=vmem << 20),
+        cost_estimate=pl.CostEstimate(flops=flops, bytes_accessed=1000000, transcendentals=0),
     )(*args)
 
 
@@ -531,16 +584,17 @@
         part_velocity,
     )
 
-    post, near, far = call(
+    post, near, far, *particles = call(
         collide_kernel,
-        (struct(20, 2, 16, 128), struct(20, 16, 128), struct(20, 16, 128)),
-        (
-            par,
-            pltpu.with_memory_space_constraint(populations, pltpu.HBM),
-            pltpu.with_memory_space_constraint(shear_rate, pltpu.HBM),
+        (struct(20, 2, 16, 128), struct(20, 16, 128), struct(20, 16, 128))
+        + tuple(jax.ShapeDtypeStruct(p.shape, p.dtype) for p in particles),
+        (par,)
+        + tuple(
+            pltpu.with_memory_space_constraint(a, pltpu.HBM)
+            for a in (populations, shear_rate, *particles)
         ),
-        [SMEM, HBM, HBM],
-        [pltpu.VMEM((19, 2, 16, 128), jnp.float32), pltpu.SemaphoreType.DMA((5,))],
+        [SMEM] + [HBM] * 7,
+        [pltpu.VMEM((19, 2, 16, 128), jnp.float32), pltpu.SemaphoreType.DMA((10,))],
     )
     xnear, xfar = both_swaps(near, far, "gx")
 
@@ -575,6 +629,13 @@
     )
     ynear, yfar = both_swaps(near, far, "gy")
 
+    field_ext, inner = call(
+        inner_kernel,
+        (struct(len(PAIRS), 16, 256), struct(19, 4, 2, 8, 256)),
+        (par, post, xnear, xfar, znear, zfar),
+        [SMEM] + [VMEM] * 5,
+        flops=20000000,
+    )
     populations_out, fluid, partial, near, far = call(
         step_kernel,
         (
@@ -584,12 +645,11 @@
             struct(4, 16, 128),
             struct(4, 16, 128),
         ),
-        (par, post, xnear, xfar, znear, zfar, ynear, yfar, *deposits),
-        [SMEM] + [VMEM] * 9,
+        (par, field_ext, inner, znear, zfar, ynear, yfar, *deposits),
+        [SMEM] + [VMEM] * 8,
         [
-            pltpu.VMEM((2, 2, 24, 128), jnp.float32),
-            pltpu.VMEM((len(PAIRS), 24, 256), jnp.float32),
-            pltpu.VMEM((19, 4, 3, 8, 256), jnp.float32),
+            pltpu.VMEM((len(PAIRS), 16, 256), jnp.float32),
+            pltpu.VMEM((19, 4, 8, 256), jnp.float32),
         ],
         flops=20000000,
     )
@@ -600,8 +660,8 @@
         drag_kernel,
         struct(3, count),
         (
-            part_cell.reshape(tall),
-            part_mask.reshape(tall),
+            particles[0].reshape(tall),
+            particles[2].reshape(tall),
             velocity_tall,
             fluid.reshape(3, 32, 128),
         ),

time: 75.7 us -> 74.5 us (0.984); the launches traced: 74.3 us -> 74.1 us
    pallas_call x9 -> x10, Pallas kernels: 14.2 us -> 14.7 us  [call(): pl.pallas_call(kernel, out_shape=outs, in_specs=specs or [VMEM] * len(arg...]
  transfers between devices with their start and end apart: 8 -> 8, of which waited for: 4 -> 4; matrix products, arithmetic and copies ran while one was open for 0% -> 0% of each run, Pallas kernels for 10% -> 12%
where the time goes in v1:
time: 74.5 us; the launch traced here: 74.1 us
  starting transfers between devices  52 us (70%)
  Pallas kernels  14.7 us (20%)
  waiting for transfers between devices  5.83 us (8%)
  other arithmetic  0.79 us (1%)
  between operations  0.79 us (1%)
    ppermute x8, starting transfers between devices, swap(): return lax.ppermute(value, axis, pairs)  52 us
    pallas_call x10, Pallas kernels, call(): pl.pallas_call(kernel, out_shape=outs, in_specs=specs or [VMEM] * len(arg...  14.7 us
    ppermute x8, waiting for transfers between devices, swap(): return lax.ppermute(value, axis, pairs)  5.83 us
  transfers between devices with their start and end apart: 8, of which 4 were waited for; matrix products, arithmetic and copies ran while one was open for 0% of the time, Pallas kernels for 12%

profile of v1, /device:TPU:6, one launch (start us, length us, event | category | flops | bytes accessed | tf_op | source)
XLA Modules:
  0.0 74.1 jit_solution(2355974481933416870)
XLA Ops:
  0.7 0.1 pad_add_fusion.par
  0.7 1.8 %shard_map.94 = (f32[20,2,16,128]{3,2,1,0:T(8,128)S(1)}, f32[20,16,128]{2,1,0:T(8,128)S(1)}, f32[20,16,128]{2,1,0:T(8,128)S(1)}, s32[1,8192]{1,0:T(1,128)S(1)}, ...) custom-call(s32[3]{0:T(128)S(1)} %pad_add_fusion.par, ...), custom_call_target="tpu_custom_call" | custom-call | flops 1000000 | bytes 1000000 | tf_op jit(solution)/shard_map/pallas_call | solution.py:564
  2.5 2.7 %collective-permute-start = (f32[20,16,128]{2,1,0:T(8,128)S(1)}, f32[20,16,128]{2,1,0:T(8,128)S(1)}, u32[]{:S(2)}, u32[]{:S(2)}) collective-permute-start(f32[20,16,128]{2,1,0:T(8,128)S(1)} %get-tuple-element.25), channel_id=1, source_target_pairs={{0,256},{256,0},{512,768},{768,512},{1,257},{257,1},{513,769},{769... | collective-permute-start | bytes 491528 | tf_op jit(solution)/shard_map/ppermute | solution.py:549
  5.3 14.2 %collective-permute-start.1 = (f32[20,16,128]{2,1,0:T(8,128)S(1)}, f32[20,16,128]{2,1,0:T(8,128)S(1)}, u32[]{:S(2)}, u32[]{:S(2)}) collective-permute-start(f32[20,16,128]{2,1,0:T(8,128)S(1)} %get-tuple-element.26), channel_id=1, source_target_pairs={{0,768},{256,512},{512,256},{768,0},{1,769},{257,513},{513,257},{7... | collective-permute-start | bytes 491528 | tf_op jit(solution)/shard_map/ppermute | solution.py:549
  19.5 0.4 shard_map.95.edge
  19.8 0.0 collective-permute-done.xnear
  19.8 2.9 %collective-permute-done.1.xfar = f32[20,16,128]{2,1,0:T(8,128)S(1)} collective-permute-done((f32[20,16,128]{2,1,0:T(8,128)S(1)}, f32[20,16,128]{2,1,0:T(8,128)S(1)}, u32[]{:S(2)}, u32[]{:S(2)}) %collective-permute-start.1) | collective-permute-done | bytes 163872 | tf_op jit(solution)/shard_map/ppermute | solution.py:549
  22.7 1.0 %shard_map.96 = (f32[2,16,128]{2,1,0:T(8,128)S(1)}, f32[2,16,128]{2,1,0:T(8,128)S(1)}) custom-call(s32[3]{0:T(128)S(1)} %pad_add_fusion.par, f32[20,2,16,128]{3,2,1,0:T(8,128)S(1)} %get-tuple-element.24.post, f32[20,16,128]{2,1,0:T(8,128)S(1)} %collective-permute-done.xnear, f32[20,16,128]{2,1,0:T(8,128)S(1)} %collective-permute-done.1.xfar, ...), custom_call_target="tpu_custom_call" | custom-call | flops 1000000 | bytes 1000000 | tf_op jit(solution)/shard_map/pallas_call | solution.py:564
  23.7 1.9 %collective-permute-start.2 = (f32[2,16,128]{2,1,0:T(8,128)S(1)}, f32[2,16,128]{2,1,0:T(8,128)S(1)}, u32[]{:S(2)}, u32[]{:S(2)}) collective-permute-start(f32[2,16,128]{2,1,0:T(8,128)S(1)} %get-tuple-element.32), channel_id=1, source_target_pairs={{0,1},{1,0},{2,3},{3,2},{4,5},{5,4},{6,7},{7,6},{8,9},{9,8},{10,11... | collective-permute-start | bytes 49160 | tf_op jit(solution)/shard_map/ppermute | solution.py:549
  25.6 7.7 %collective-permute-start.3 = (f32[2,16,128]{2,1,0:T(8,128)S(1)}, f32[2,16,128]{2,1,0:T(8,128)S(1)}, u32[]{:S(2)}, u32[]{:S(2)}) collective-permute-start(f32[2,16,128]{2,1,0:T(8,128)S(1)} %get-tuple-element.33), channel_id=1, source_target_pairs={{0,15},{1,2},{2,1},{3,4},{4,3},{5,6},{6,5},{7,8},{8,7},{9,10},{10,... | collective-permute-start | bytes 49160 | tf_op jit(solution)/shard_map/ppermute | solution.py:549
  33.4 2.4 %shard_map.100 = f32[2,256,128]{2,1,0:T(8,128)S(1)} custom-call(s32[1,8192]{1,0:T(1,128)S(1)} %get-tuple-element.27.cell, s32[1,8192]{1,0:T(1,128)S(1)} %get-tuple-element.28.move, s32[1,8192]{1,0:T(1,128)S(1)} %get-tuple-element.29.mask, f32[1,8192]{1,0:T(1,128)S(1)} %get-tuple-element.30.mass, f32[3,8192]{1,0:T(4,128)S(1)} %get-tuple-element.31.velocity), custom_call_target="tpu_custom_call" | custom-call | flops 2000000000 | bytes 1000000 | tf_op jit(solution)/shard_map/pallas_call | solution.py:564
  35.8 0.8 %shard_map.98 = (f32[16,128]{1,0:T(8,128)S(1)}, f32[3,64,128]{2,1,0:T(8,128)S(1)}) custom-call(s32[1,8192]{1,0:T(1,128)S(1)} %get-tuple-element.27.cell, s32[1,8192]{1,0:T(1,128)S(1)} %get-tuple-element.28.move, s32[1,8192]{1,0:T(1,128)S(1)} %get-tuple-element.29.mask, f32[1,8192]{1,0:T(1,128)S(1)} %get-tuple-element.30.mass, ...), custom_call_target="tpu_custom_call" | custom-call | flops 1000000 | bytes 1000000 | tf_op jit(solution)/shard_map/pallas_call | solution.py:564
  36.6 0.0 collective-permute-done.2.znear
  36.6 0.8 %collective-permute-done.3.zfar = f32[2,16,128]{2,1,0:T(8,128)S(1)} collective-permute-done((f32[2,16,128]{2,1,0:T(8,128)S(1)}, f32[2,16,128]{2,1,0:T(8,128)S(1)}, u32[]{:S(2)}, u32[]{:S(2)}) %collective-permute-start.3) | collective-permute-done | bytes 16416 | tf_op jit(solution)/shard_map/ppermute | solution.py:549
  37.3 0.6 shard_map.99
  37.9 2.7 %collective-permute-start.4 = (f32[264,128]{1,0:T(8,128)S(1)}, f32[264,128]{1,0:T(8,128)S(1)}, u32[]{:S(2)}, u32[]{:S(2)}) collective-permute-start(f32[264,128]{1,0:T(8,128)S(1)} %get-tuple-element.37), channel_id=1, source_target_pairs={{0,16},{16,0},{32,48},{48,32},{64,80},{80,64},{96,112},{112,96},{1... | collective-permute-start | bytes 405512 | tf_op jit(solution)/shard_map/ppermute | solution.py:549
  40.7 14.5 %collective-permute-start.5 = (f32[264,128]{1,0:T(8,128)S(1)}, f32[264,128]{1,0:T(8,128)S(1)}, u32[]{:S(2)}, u32[]{:S(2)}) collective-permute-start(f32[264,128]{1,0:T(8,128)S(1)} %get-tuple-element.38), channel_id=1, source_target_pairs={{0,240},{16,32},{32,16},{48,64},{64,48},{80,96},{96,80},{112,128},... | collective-permute-start | bytes 405512 | tf_op jit(solution)/shard_map/ppermute | solution.py:549
  55.2 2.4 %shard_map.101 = f32[2,256,128]{2,1,0:T(8,128)S(1)} custom-call(s32[1,8192]{1,0:T(1,128)S(1)} %get-tuple-element.27.cell, s32[1,8192]{1,0:T(1,128)S(1)} %get-tuple-element.28.move, s32[1,8192]{1,0:T(1,128)S(1)} %get-tuple-element.29.mask, f32[1,8192]{1,0:T(1,128)S(1)} %get-tuple-element.30.mass, f32[3,8192]{1,0:T(4,128)S(1)} %get-tuple-element.31.velocity), custom_call_target="tpu_custom_call" | custom-call | flops 2000000000 | bytes 1000000 | tf_op jit(solution)/shard_map/pallas_call | solution.py:564
  57.6 1.7 %shard_map.97 = (f32[80,16,256]{2,1,0:T(8,128)S(1)}, f32[19,4,2,8,256]{4,3,2,1,0:T(8,128)S(1)}) custom-call(s32[3]{0:T(128)S(1)} %pad_add_fusion.par, f32[20,2,16,128]{3,2,1,0:T(8,128)S(1)} %get-tuple-element.24.post, f32[20,16,128]{2,1,0:T(8,128)S(1)} %collective-permute-done.xnear, f32[20,16,128]{2,1,0:T(8,128)S(1)} %collective-permute-done.1.xfar, ...), custom_call_target="tpu_custom_call" | custom-call | flops 20000000 | bytes 1000000 | tf_op jit(solution)/shard_map/pallas_call | solution.py:564
  59.3 0.0 collective-permute-done.4.ynear
  59.3 0.3 collective-permute-done.5.yfar
  59.7 2.1 %shard_map.102 = (f32[19,2,16,128]{3,2,1,0:T(8,128)}, f32[3,2,16,128]{3,2,1,0:T(8,128)S(1)}, f32[4,2,16,128]{3,2,1,0:T(8,128)S(1)}, f32[4,16,128]{2,1,0:T(8,128)S(1)}, f32[4,16,128]{2,1,0:T(8,128)S(1)}) custom-call(s32[3]{0:T(128)S(1)} %pad_add_fusion.par, f32[80,16,256]{2,1,0:T(8,128)S(1)} %get-tuple-element.34.field_ext, ...), custom_call_target="tpu_custom_call" | custom-call | flops 20000000 | bytes 1000000 | tf_op jit(solution)/shard_map/pallas_call | solution.py:564
  61.8 5.8 %collective-permute-start.7 = (f32[4,16,128]{2,1,0:T(8,128)S(1)}, f32[4,16,128]{2,1,0:T(8,128)S(1)}, u32[]{:S(2)}, u32[]{:S(2)}) collective-permute-start(f32[4,16,128]{2,1,0:T(8,128)S(1)} %get-tuple-element.42), channel_id=1, source_target_pairs={{0,768},{256,512},{512,256},{768,0},{1,769},{257,513},{513,257},{7... | collective-permute-start | bytes 98312 | tf_op jit(solution)/shard_map/ppermute | solution.py:549
  67.6 2.4 %collective-permute-start.6 = (f32[4,16,128]{2,1,0:T(8,128)S(1)}, f32[4,16,128]{2,1,0:T(8,128)S(1)}, u32[]{:S(2)}, u32[]{:S(2)}) collective-permute-start(f32[4,16,128]{2,1,0:T(8,128)S(1)} %get-tuple-element.41), channel_id=1, source_target_pairs={{0,256},{256,0},{512,768},{768,512},{1,257},{257,1},{513,769},{769... | collective-permute-start | bytes 98312 | tf_op jit(solution)/shard_map/ppermute | solution.py:549
  70.0 1.6 %shard_map.103 = f32[3,8192]{1,0:T(4,128)} custom-call(s32[64,128]{1,0:T(8,128)S(1)} %bitcast.12, s32[64,128]{1,0:T(8,128)S(1)} %bitcast.13, f32[3,64,128]{2,1,0:T(8,128)S(1)} %get-tuple-element.43.velocity, f32[3,32,128]{2,1,0:T(8,128)S(1)} %bitcast.16), custom_call_target="tpu_custom_call" | custom-call | flops 1000000 | bytes 1000000 | tf_op jit(solution)/shard_map/pallas_call | solution.py:564
  71.6 0.0 collective-permute-done.7
  71.6 1.8 %collective-permute-done.6 = f32[4,16,128]{2,1,0:T(8,128)S(1)} collective-permute-done((f32[4,16,128]{2,1,0:T(8,128)S(1)}, f32[4,16,128]{2,1,0:T(8,128)S(1)}, u32[]{:S(2)}, u32[]{:S(2)}) %collective-permute-start.6) | collective-permute-done | bytes 32800 | tf_op jit(solution)/shard_map/ppermute | solution.py:549
  73.4 0.7 select_add_fusion
  (1 shorter events, 0.0 us)
Async XLA Ops:
  2.5 17.3 %collective-permute-start = (f32[20,16,128]{2,1,0:T(8,128)S(1)}, f32[20,16,128]{2,1,0:T(8,128)S(1)}, u32[]{:S(2)}, u32[]{:S(2)}) collective-permute-start(f32[20,16,128]{2,1,0:T(8,128)S(1)} %get-tuple-element.25), channel_id=1, source_target_pairs={{0,256},{256,0},{512,768},{768,512},{1,257},{257,1},{513,769},{769... | collective-permute-start | bytes 491528 | tf_op jit(solution)/shard_map/ppermute | solution.py:549
  5.3 17.5 %collective-permute-start.1 = (f32[20,16,128]{2,1,0:T(8,128)S(1)}, f32[20,16,128]{2,1,0:T(8,128)S(1)}, u32[]{:S(2)}, u32[]{:S(2)}) collective-permute-start(f32[20,16,128]{2,1,0:T(8,128)S(1)} %get-tuple-element.26), channel_id=1, source_target_pairs={{0,768},{256,512},{512,256},{768,0},{1,769},{257,513},{513,257},{7... | collective-permute-start | bytes 491528 | tf_op jit(solution)/shard_map/ppermute | solution.py:549
  23.7 12.8 %collective-permute-start.2 = (f32[2,16,128]{2,1,0:T(8,128)S(1)}, f32[2,16,128]{2,1,0:T(8,128)S(1)}, u32[]{:S(2)}, u32[]{:S(2)}) collective-permute-start(f32[2,16,128]{2,1,0:T(8,128)S(1)} %get-tuple-element.32), channel_id=1, source_target_pairs={{0,1},{1,0},{2,3},{3,2},{4,5},{5,4},{6,7},{7,6},{8,9},{9,8},{10,11... | collective-permute-start | bytes 49160 | tf_op jit(solution)/shard_map/ppermute | solution.py:549
  25.6 11.7 %collective-permute-start.3 = (f32[2,16,128]{2,1,0:T(8,128)S(1)}, f32[2,16,128]{2,1,0:T(8,128)S(1)}, u32[]{:S(2)}, u32[]{:S(2)}) collective-permute-start(f32[2,16,128]{2,1,0:T(8,128)S(1)} %get-tuple-element.33), channel_id=1, source_target_pairs={{0,15},{1,2},{2,1},{3,4},{4,3},{5,6},{6,5},{7,8},{8,7},{9,10},{10,... | collective-permute-start | bytes 49160 | tf_op jit(solution)/shard_map/ppermute | solution.py:549
  37.9 21.4 %collective-permute-start.4 = (f32[264,128]{1,0:T(8,128)S(1)}, f32[264,128]{1,0:T(8,128)S(1)}, u32[]{:S(2)}, u32[]{:S(2)}) collective-permute-start(f32[264,128]{1,0:T(8,128)S(1)} %get-tuple-element.37), channel_id=1, source_target_pairs={{0,16},{16,0},{32,48},{48,32},{64,80},{80,64},{96,112},{112,96},{1... | collective-permute-start | bytes 405512 | tf_op jit(solution)/shard_map/ppermute | solution.py:549
  40.7 19.0 %collective-permute-start.5 = (f32[264,128]{1,0:T(8,128)S(1)}, f32[264,128]{1,0:T(8,128)S(1)}, u32[]{:S(2)}, u32[]{:S(2)}) collective-permute-start(f32[264,128]{1,0:T(8,128)S(1)} %get-tuple-element.38), channel_id=1, source_target_pairs={{0,240},{16,32},{32,16},{48,64},{64,48},{80,96},{96,80},{112,128},... | collective-permute-start | bytes 405512 | tf_op jit(solution)/shard_map/ppermute | solution.py:549
  61.8 9.7 %collective-permute-start.7 = (f32[4,16,128]{2,1,0:T(8,128)S(1)}, f32[4,16,128]{2,1,0:T(8,128)S(1)}, u32[]{:S(2)}, u32[]{:S(2)}) collective-permute-start(f32[4,16,128]{2,1,0:T(8,128)S(1)} %get-tuple-element.42), channel_id=1, source_target_pairs={{0,768},{256,512},{512,256},{768,0},{1,769},{257,513},{513,257},{7... | collective-permute-start | bytes 98312 | tf_op jit(solution)/shard_map/ppermute | solution.py:549
  67.6 5.8 %collective-permute-start.6 = (f32[4,16,128]{2,1,0:T(8,128)S(1)}, f32[4,16,128]{2,1,0:T(8,128)S(1)}, u32[]{:S(2)}, u32[]{:S(2)}) collective-permute-start(f32[4,16,128]{2,1,0:T(8,128)S(1)} %get-tuple-element.41), channel_id=1, source_target_pairs={{0,256},{256,0},{512,768},{768,512},{1,257},{257,1},{513,769},{769... | collective-permute-start | bytes 98312 | tf_op jit(solution)/shard_map/ppermute | solution.py:549

commit v2 on v1

--- a/solution.py
+++ b/solution.py
@@ -167,18 +167,33 @@
     return main
 
 
-def z_pack_kernel(par, post, xnear, xfar, edge, near, far):
-    main = reader(par, post, xnear, xfar)
+def place_columns(tile, pairs, value_of, high, low):
+    lane = lax.broadcasted_iota(jnp.int32, (16, 128), 1)
+    for q in pairs:
+        if (q < FIRST) == (tile == 0):
+            slot = q - tile * FIRST
+            value = value_of(q)
+            mine = (lane >= 3 * slot) & (lane < 3 * slot + 3)
+            high = jnp.where(mine, pltpu.roll(value, (3 * slot + 3) % 128, 1), high)
+            low = jnp.where(mine, pltpu.roll(value, 3 * slot, 1), low)
+    return high, low
+
+
+def z_own_kernel(post, own):
+    zero = jnp.zeros((16, 128), jnp.float32)
+    for tile in range(2):
+        own[0, tile], own[1, tile] = place_columns(
+            tile, range(20, 60), lambda q: post[PAIRS[q][0], PAIRS[q][1]], zero, zero
+        )
+
+
+def z_pack_kernel(par, own, xnear, xfar, edge, near, far):
+    main = reader(par, None, xnear, xfar)
     even = par[2] == 0
     lane = lax.broadcasted_iota(jnp.int32, (16, 128), 1)
     for tile in range(2):
-        high = jnp.zeros((16, 128), jnp.float32)
-        low = jnp.zeros((16, 128), jnp.float32)
-        for slot in range(FIRST if tile == 0 else len(PAIRS) - FIRST):
-            value = main(tile * FIRST + slot)
-            mine = (lane >= 3 * slot) & (lane < 3 * slot + 3)
-            high = jnp.where(mine, pltpu.roll(value, (3 * slot + 3) % 128, 1), high)
-            low = jnp.where(mine, pltpu.roll(value, 3 * slot, 1), low)
+        ghosts = (*range(20), *range(60, 80))
+        high, low = place_columns(tile, ghosts, main, own[0, tile], own[1, tile])
         if tile == 1:
             sums = edge[...] + pltpu.roll(edge[...], 112, 1)
             odd = jnp.bitwise_and(lane - DEP_LANE, 1) == 1
@@ -599,10 +614,11 @@
     xnear, xfar = both_swaps(near, far, "gx")
 
     edge = call(z_edge_kernel, struct(32, 128), particles)
+    own = call(z_own_kernel, struct(2, 2, 16, 128), (post,))
     near, far = call(
         z_pack_kernel,
         (struct(2, 16, 128), struct(2, 16, 128)),
-        (par, post, xnear, xfar, edge),
+        (par, own, xnear, xfar, edge),
         [SMEM] + [VMEM] * 4,
     )
     znear, zfar = both_swaps(near, far, "gz")

time: 74.5 us -> 74.3 us (level)
    pallas_call x10 -> x11, Pallas kernels: 14.7 us -> 14.8 us  [call(): pl.pallas_call(kernel, out_shape=outs, in_specs=specs or [VMEM] * len(arg...]
  transfers between devices with their start and end apart: 8 -> 8, of which waited for: 4 -> 4; matrix products, arithmetic and copies ran while one was open for 0% -> 0% of each run, Pallas kernels for 12% -> 13%
where the time goes in v2:
time: 74.3 us; the launch traced here: 73.9 us
  starting transfers between devices  52 us (70%)
  Pallas kernels  14.8 us (20%)
  waiting for transfers between devices  5.61 us (8%)
  other arithmetic  0.79 us (1%)
  between operations  0.79 us (1%)
    ppermute x8, starting transfers between devices, swap(): return lax.ppermute(value, axis, pairs)  52 us
    pallas_call x11, Pallas kernels, call(): pl.pallas_call(kernel, out_shape=outs, in_specs=specs or [VMEM] * len(arg...  14.8 us
    ppermute x8, waiting for transfers between devices, swap(): return lax.ppermute(value, axis, pairs)  5.61 us
  transfers between devices with their start and end apart: 8, of which 4 were waited for; matrix products, arithmetic and copies ran while one was open for 0% of the time, Pallas kernels for 13%

profile of v2, /device:TPU:6, one launch (start us, length us, event | category | flops | bytes accessed | tf_op | source)
XLA Modules:
  0.0 73.9 jit_solution(4875455774813876694)
XLA Ops:
  0.7 0.1 pad_add_fusion.par
  0.7 1.8 %shard_map.94 = (f32[20,2,16,128]{3,2,1,0:T(8,128)S(1)}, f32[20,16,128]{2,1,0:T(8,128)S(1)}, f32[20,16,128]{2,1,0:T(8,128)S(1)}, s32[1,8192]{1,0:T(1,128)S(1)}, ...) custom-call(s32[3]{0:T(128)S(1)} %pad_add_fusion.par, ...), custom_call_target="tpu_custom_call" | custom-call | flops 1000000 | bytes 1000000 | tf_op jit(solution)/shard_map/pallas_call | solution.py:579
  2.5 2.7 %collective-permute-start = (f32[20,16,128]{2,1,0:T(8,128)S(1)}, f32[20,16,128]{2,1,0:T(8,128)S(1)}, u32[]{:S(2)}, u32[]{:S(2)}) collective-permute-start(f32[20,16,128]{2,1,0:T(8,128)S(1)} %get-tuple-element.25), channel_id=1, source_target_pairs={{0,256},{256,0},{512,768},{768,512},{1,257},{257,1},{513,769},{769... | collective-permute-start | bytes 491528 | tf_op jit(solution)/shard_map/ppermute | solution.py:564
  5.3 14.2 %collective-permute-start.1 = (f32[20,16,128]{2,1,0:T(8,128)S(1)}, f32[20,16,128]{2,1,0:T(8,128)S(1)}, u32[]{:S(2)}, u32[]{:S(2)}) collective-permute-start(f32[20,16,128]{2,1,0:T(8,128)S(1)} %get-tuple-element.26), channel_id=1, source_target_pairs={{0,768},{256,512},{512,256},{768,0},{1,769},{257,513},{513,257},{7... | collective-permute-start | bytes 491528 | tf_op jit(solution)/shard_map/ppermute | solution.py:564
  19.5 0.2 shard_map.95.own
  19.7 0.4 shard_map.96.edge
  20.1 0.0 collective-permute-done.xnear
  20.1 2.7 %collective-permute-done.1.xfar = f32[20,16,128]{2,1,0:T(8,128)S(1)} collective-permute-done((f32[20,16,128]{2,1,0:T(8,128)S(1)}, f32[20,16,128]{2,1,0:T(8,128)S(1)}, u32[]{:S(2)}, u32[]{:S(2)}) %collective-permute-start.1) | collective-permute-done | bytes 163872 | tf_op jit(solution)/shard_map/ppermute | solution.py:564
  22.7 0.8 %shard_map.97 = (f32[2,16,128]{2,1,0:T(8,128)S(1)}, f32[2,16,128]{2,1,0:T(8,128)S(1)}) custom-call(s32[3]{0:T(128)S(1)} %pad_add_fusion.par, f32[2,2,16,128]{3,2,1,0:T(8,128)S(1)} %shard_map.95.own, f32[20,16,128]{2,1,0:T(8,128)S(1)} %collective-permute-done.xnear, f32[20,16,128]{2,1,0:T(8,128)S(1)} %collective-permute-done.1.xfar, f32[32,128]{1,0:T(8,128)S(1)} %shard_map.96.edge), custom_call_target="tpu_custom_call" | custom-call | flops 1000000 | bytes 1000000 | tf_op jit(solution)/shard_map/pallas_call | solution.py:579
  23.5 1.9 %collective-permute-start.2 = (f32[2,16,128]{2,1,0:T(8,128)S(1)}, f32[2,16,128]{2,1,0:T(8,128)S(1)}, u32[]{:S(2)}, u32[]{:S(2)}) collective-permute-start(f32[2,16,128]{2,1,0:T(8,128)S(1)} %get-tuple-element.32), channel_id=1, source_target_pairs={{0,1},{1,0},{2,3},{3,2},{4,5},{5,4},{6,7},{7,6},{8,9},{9,8},{10,11... | collective-permute-start | bytes 49160 | tf_op jit(solution)/shard_map/ppermute | solution.py:564
  25.5 7.7 %collective-permute-start.3 = (f32[2,16,128]{2,1,0:T(8,128)S(1)}, f32[2,16,128]{2,1,0:T(8,128)S(1)}, u32[]{:S(2)}, u32[]{:S(2)}) collective-permute-start(f32[2,16,128]{2,1,0:T(8,128)S(1)} %get-tuple-element.33), channel_id=1, source_target_pairs={{0,15},{1,2},{2,1},{3,4},{4,3},{5,6},{6,5},{7,8},{8,7},{9,10},{10,... | collective-permute-start | bytes 49160 | tf_op jit(solution)/shard_map/ppermute | solution.py:564
  33.2 2.4 %shard_map.101 = f32[2,256,128]{2,1,0:T(8,128)S(1)} custom-call(s32[1,8192]{1,0:T(1,128)S(1)} %get-tuple-element.27.cell, s32[1,8192]{1,0:T(1,128)S(1)} %get-tuple-element.28.move, s32[1,8192]{1,0:T(1,128)S(1)} %get-tuple-element.29.mask, f32[1,8192]{1,0:T(1,128)S(1)} %get-tuple-element.30.mass, f32[3,8192]{1,0:T(4,128)S(1)} %get-tuple-element.31.velocity), custom_call_target="tpu_custom_call" | custom-call | flops 2000000000 | bytes 1000000 | tf_op jit(solution)/shard_map/pallas_call | solution.py:579
  35.6 0.8 %shard_map.99 = (f32[16,128]{1,0:T(8,128)S(1)}, f32[3,64,128]{2,1,0:T(8,128)S(1)}) custom-call(s32[1,8192]{1,0:T(1,128)S(1)} %get-tuple-element.27.cell, s32[1,8192]{1,0:T(1,128)S(1)} %get-tuple-element.28.move, s32[1,8192]{1,0:T(1,128)S(1)} %get-tuple-element.29.mask, f32[1,8192]{1,0:T(1,128)S(1)} %get-tuple-element.30.mass, ...), custom_call_target="tpu_custom_call" | custom-call | flops 1000000 | bytes 1000000 | tf_op jit(solution)/shard_map/pallas_call | solution.py:579
  36.4 0.0 collective-permute-done.2.znear
  36.4 0.8 %collective-permute-done.3.zfar = f32[2,16,128]{2,1,0:T(8,128)S(1)} collective-permute-done((f32[2,16,128]{2,1,0:T(8,128)S(1)}, f32[2,16,128]{2,1,0:T(8,128)S(1)}, u32[]{:S(2)}, u32[]{:S(2)}) %collective-permute-start.3) | collective-permute-done | bytes 16416 | tf_op jit(solution)/shard_map/ppermute | solution.py:564
  37.1 0.6 shard_map.100
  37.7 2.7 %collective-permute-start.4 = (f32[264,128]{1,0:T(8,128)S(1)}, f32[264,128]{1,0:T(8,128)S(1)}, u32[]{:S(2)}, u32[]{:S(2)}) collective-permute-start(f32[264,128]{1,0:T(8,128)S(1)} %get-tuple-element.37), channel_id=1, source_target_pairs={{0,16},{16,0},{32,48},{48,32},{64,80},{80,64},{96,112},{112,96},{1... | collective-permute-start | bytes 405512 | tf_op jit(solution)/shard_map/ppermute | solution.py:564
  40.5 14.5 %collective-permute-start.5 = (f32[264,128]{1,0:T(8,128)S(1)}, f32[264,128]{1,0:T(8,128)S(1)}, u32[]{:S(2)}, u32[]{:S(2)}) collective-permute-start(f32[264,128]{1,0:T(8,128)S(1)} %get-tuple-element.38), channel_id=1, source_target_pairs={{0,240},{16,32},{32,16},{48,64},{64,48},{80,96},{96,80},{112,128},... | collective-permute-start | bytes 405512 | tf_op jit(solution)/shard_map/ppermute | solution.py:564
  55.0 2.4 %shard_map.102 = f32[2,256,128]{2,1,0:T(8,128)S(1)} custom-call(s32[1,8192]{1,0:T(1,128)S(1)} %get-tuple-element.27.cell, s32[1,8192]{1,0:T(1,128)S(1)} %get-tuple-element.28.move, s32[1,8192]{1,0:T(1,128)S(1)} %get-tuple-element.29.mask, f32[1,8192]{1,0:T(1,128)S(1)} %get-tuple-element.30.mass, f32[3,8192]{1,0:T(4,128)S(1)} %get-tuple-element.31.velocity), custom_call_target="tpu_custom_call" | custom-call | flops 2000000000 | bytes 1000000 | tf_op jit(solution)/shard_map/pallas_call | solution.py:579
  57.4 1.7 %shard_map.98 = (f32[80,16,256]{2,1,0:T(8,128)S(1)}, f32[19,4,2,8,256]{4,3,2,1,0:T(8,128)S(1)}) custom-call(s32[3]{0:T(128)S(1)} %pad_add_fusion.par, f32[20,2,16,128]{3,2,1,0:T(8,128)S(1)} %get-tuple-element.24.post, f32[20,16,128]{2,1,0:T(8,128)S(1)} %collective-permute-done.xnear, f32[20,16,128]{2,1,0:T(8,128)S(1)} %collective-permute-done.1.xfar, ...), custom_call_target="tpu_custom_call" | custom-call | flops 20000000 | bytes 1000000 | tf_op jit(solution)/shard_map/pallas_call | solution.py:579
  59.1 0.0 collective-permute-done.4.ynear
  59.1 0.3 collective-permute-done.5.yfar
  59.5 2.1 %shard_map.103 = (f32[19,2,16,128]{3,2,1,0:T(8,128)}, f32[3,2,16,128]{3,2,1,0:T(8,128)S(1)}, f32[4,2,16,128]{3,2,1,0:T(8,128)S(1)}, f32[4,16,128]{2,1,0:T(8,128)S(1)}, f32[4,16,128]{2,1,0:T(8,128)S(1)}) custom-call(s32[3]{0:T(128)S(1)} %pad_add_fusion.par, f32[80,16,256]{2,1,0:T(8,128)S(1)} %get-tuple-element.34.field_ext, ...), custom_call_target="tpu_custom_call" | custom-call | flops 20000000 | bytes 1000000 | tf_op jit(solution)/shard_map/pallas_call | solution.py:579
  61.6 5.8 %collective-permute-start.7 = (f32[4,16,128]{2,1,0:T(8,128)S(1)}, f32[4,16,128]{2,1,0:T(8,128)S(1)}, u32[]{:S(2)}, u32[]{:S(2)}) collective-permute-start(f32[4,16,128]{2,1,0:T(8,128)S(1)} %get-tuple-element.42), channel_id=1, source_target_pairs={{0,768},{256,512},{512,256},{768,0},{1,769},{257,513},{513,257},{7... | collective-permute-start | bytes 98312 | tf_op jit(solution)/shard_map/ppermute | solution.py:564
  67.4 2.4 %collective-permute-start.6 = (f32[4,16,128]{2,1,0:T(8,128)S(1)}, f32[4,16,128]{2,1,0:T(8,128)S(1)}, u32[]{:S(2)}, u32[]{:S(2)}) collective-permute-start(f32[4,16,128]{2,1,0:T(8,128)S(1)} %get-tuple-element.41), channel_id=1, source_target_pairs={{0,256},{256,0},{512,768},{768,512},{1,257},{257,1},{513,769},{769... | collective-permute-start | bytes 98312 | tf_op jit(solution)/shard_map/ppermute | solution.py:564
  69.8 1.6 %shard_map.104 = f32[3,8192]{1,0:T(4,128)} custom-call(s32[64,128]{1,0:T(8,128)S(1)} %bitcast.12, s32[64,128]{1,0:T(8,128)S(1)} %bitcast.13, f32[3,64,128]{2,1,0:T(8,128)S(1)} %get-tuple-element.43.velocity, f32[3,32,128]{2,1,0:T(8,128)S(1)} %bitcast.16), custom_call_target="tpu_custom_call" | custom-call | flops 1000000 | bytes 1000000 | tf_op jit(solution)/shard_map/pallas_call | solution.py:579
  71.4 0.0 collective-permute-done.7
  71.4 1.8 %collective-permute-done.6 = f32[4,16,128]{2,1,0:T(8,128)S(1)} collective-permute-done((f32[4,16,128]{2,1,0:T(8,128)S(1)}, f32[4,16,128]{2,1,0:T(8,128)S(1)}, u32[]{:S(2)}, u32[]{:S(2)}) %collective-permute-start.6) | collective-permute-done | bytes 32800 | tf_op jit(solution)/shard_map/ppermute | solution.py:564
  73.2 0.7 select_add_fusion
  (1 shorter events, 0.0 us)
Async XLA Ops:
  2.5 17.6 %collective-permute-start = (f32[20,16,128]{2,1,0:T(8,128)S(1)}, f32[20,16,128]{2,1,0:T(8,128)S(1)}, u32[]{:S(2)}, u32[]{:S(2)}) collective-permute-start(f32[20,16,128]{2,1,0:T(8,128)S(1)} %get-tuple-element.25), channel_id=1, source_target_pairs={{0,256},{256,0},{512,768},{768,512},{1,257},{257,1},{513,769},{769... | collective-permute-start | bytes 491528 | tf_op jit(solution)/shard_map/ppermute | solution.py:564
  5.3 17.5 %collective-permute-start.1 = (f32[20,16,128]{2,1,0:T(8,128)S(1)}, f32[20,16,128]{2,1,0:T(8,128)S(1)}, u32[]{:S(2)}, u32[]{:S(2)}) collective-permute-start(f32[20,16,128]{2,1,0:T(8,128)S(1)} %get-tuple-element.26), channel_id=1, source_target_pairs={{0,768},{256,512},{512,256},{768,0},{1,769},{257,513},{513,257},{7... | collective-permute-start | bytes 491528 | tf_op jit(solution)/shard_map/ppermute | solution.py:564
  23.5 12.8 %collective-permute-start.2 = (f32[2,16,128]{2,1,0:T(8,128)S(1)}, f32[2,16,128]{2,1,0:T(8,128)S(1)}, u32[]{:S(2)}, u32[]{:S(2)}) collective-permute-start(f32[2,16,128]{2,1,0:T(8,128)S(1)} %get-tuple-element.32), channel_id=1, source_target_pairs={{0,1},{1,0},{2,3},{3,2},{4,5},{5,4},{6,7},{7,6},{8,9},{9,8},{10,11... | collective-permute-start | bytes 49160 | tf_op jit(solution)/shard_map/ppermute | solution.py:564
  25.5 11.7 %collective-permute-start.3 = (f32[2,16,128]{2,1,0:T(8,128)S(1)}, f32[2,16,128]{2,1,0:T(8,128)S(1)}, u32[]{:S(2)}, u32[]{:S(2)}) collective-permute-start(f32[2,16,128]{2,1,0:T(8,128)S(1)} %get-tuple-element.33), channel_id=1, source_target_pairs={{0,15},{1,2},{2,1},{3,4},{4,3},{5,6},{6,5},{7,8},{8,7},{9,10},{10,... | collective-permute-start | bytes 49160 | tf_op jit(solution)/shard_map/ppermute | solution.py:564
  37.7 21.4 %collective-permute-start.4 = (f32[264,128]{1,0:T(8,128)S(1)}, f32[264,128]{1,0:T(8,128)S(1)}, u32[]{:S(2)}, u32[]{:S(2)}) collective-permute-start(f32[264,128]{1,0:T(8,128)S(1)} %get-tuple-element.37), channel_id=1, source_target_pairs={{0,16},{16,0},{32,48},{48,32},{64,80},{80,64},{96,112},{112,96},{1... | collective-permute-start | bytes 405512 | tf_op jit(solution)/shard_map/ppermute | solution.py:564
  40.5 19.0 %collective-permute-start.5 = (f32[264,128]{1,0:T(8,128)S(1)}, f32[264,128]{1,0:T(8,128)S(1)}, u32[]{:S(2)}, u32[]{:S(2)}) collective-permute-start(f32[264,128]{1,0:T(8,128)S(1)} %get-tuple-element.38), channel_id=1, source_target_pairs={{0,240},{16,32},{32,16},{48,64},{64,48},{80,96},{96,80},{112,128},... | collective-permute-start | bytes 405512 | tf_op jit(solution)/shard_map/ppermute | solution.py:564
  61.6 9.7 %collective-permute-start.7 = (f32[4,16,128]{2,1,0:T(8,128)S(1)}, f32[4,16,128]{2,1,0:T(8,128)S(1)}, u32[]{:S(2)}, u32[]{:S(2)}) collective-permute-start(f32[4,16,128]{2,1,0:T(8,128)S(1)} %get-tuple-element.42), channel_id=1, source_target_pairs={{0,768},{256,512},{512,256},{768,0},{1,769},{257,513},{513,257},{7... | collective-permute-start | bytes 98312 | tf_op jit(solution)/shard_map/ppermute | solution.py:564
  67.4 5.8 %collective-permute-start.6 = (f32[4,16,128]{2,1,0:T(8,128)S(1)}, f32[4,16,128]{2,1,0:T(8,128)S(1)}, u32[]{:S(2)}, u32[]{:S(2)}) collective-permute-start(f32[4,16,128]{2,1,0:T(8,128)S(1)} %get-tuple-element.41), channel_id=1, source_target_pairs={{0,256},{256,0},{512,768},{768,512},{1,257},{257,1},{513,769},{769... | collective-permute-start | bytes 98312 | tf_op jit(solution)/shard_map/ppermute | solution.py:564
